TPU v7x, 256 devices: a whole 4x4x8 slice. The times are simulated.
256 devices in a mesh: mode: 16 (over x_hi, y, core), site: 16 (over z, x_lo).
Axes of the slice: x: 4 (x_hi: 2, x_lo: 2; x = x_hi * 2 + x_lo), y: 4, z: 8, core: 2. Of those that a mesh axis runs over, the one named last changes fastest.
Arguments:
- eigvecs: bfloat16 [2, 64, 3, 110592], P(None, 'mode', None, 'site'), may hold values from -6 to 6
- perams: bfloat16 [2, 16, 64, 64], replicated, may hold values from -0.75 to 0.75
- momenta: int32 [2, 3], replicated, may hold values from -2 to 2
- spins: int32 [16, 3], replicated, may hold values from 0 to 15
- pair_combs: int32 [16, 2], P('site'), may hold values from 0 to 15
- pair_moms: int32 [16, 2], P('site'), may hold values from 0 to 1
Outputs:
- exchange: float32 [16, 2, 64, 64], P('site', None, 'mode')
All inputs are finite; a program needn't handle non-finite values.
Results may differ from a plain program's by a relative error of at most 0.018.
Values may be sent and summed in bfloat16 or wider, within the bound.
No kernel may reach another device: no remote copies, remote signals or barrier semaphores. Data moves between devices by JAX's collectives and lax.ppermute only.
A program may use at most 64 MiB of HBM per device.

v0:
```python
import jax
import jax.numpy as jnp
from jax import lax
from jax.sharding import PartitionSpec as P

LAT = 48


def hartley(momenta, glob):
    coord_x = glob // (LAT * LAT)
    coord_y = glob // LAT % LAT
    coord_z = glob % LAT
    wave = (
        momenta[:, 0:1] * coord_x[None]
        + momenta[:, 1:2] * coord_y[None]
        + momenta[:, 2:3] * coord_z[None]
    ) % LAT
    theta = wave.astype(jnp.float32) * (2.0 * jnp.pi / LAT)
    return jnp.cos(theta) + jnp.sin(theta)


def body(eigvecs, perams, momenta, spins, pair_combs, pair_moms):
    nslice, mode_dev, _, site_dev = eigvecs.shape
    nmode = perams.shape[-1]
    nspin = perams.shape[1]
    ncomb = spins.shape[0]
    nmom = momenta.shape[0]
    comb_dev = ncomb // lax.axis_size("site")
    first_mode = lax.axis_index("mode") * mode_dev
    gathered = lax.all_gather(eigvecs, "mode", axis=1, tiled=True)
    glob = lax.axis_index("site") * site_dev + jnp.arange(site_dev, dtype=jnp.int32)
    phase = hartley(momenta, glob)

    def triplet_part(vectors):
        floats = vectors.astype(jnp.float32)
        own_modes = lax.dynamic_slice_in_dim(floats, first_mode, mode_dev, 0)
        left = own_modes[:, None]
        right = floats[None]
        cross_0 = left[:, :, 1] * right[:, :, 2] - left[:, :, 2] * right[:, :, 1]
        cross_1 = left[:, :, 2] * right[:, :, 0] - left[:, :, 0] * right[:, :, 2]
        cross_2 = left[:, :, 0] * right[:, :, 1] - left[:, :, 1] * right[:, :, 0]
        diquark = jnp.stack([cross_0, cross_1, cross_2], axis=2).astype(jnp.bfloat16)
        weighted = (phase[:, None, None, :] * floats[None]).astype(jnp.bfloat16)
        product = lax.dot_general(
            diquark.reshape(mode_dev * nmode, 3 * site_dev),
            weighted.reshape(nmom * nmode, 3 * site_dev),
            (((1,), (1,)), ((), ())),
            preferred_element_type=jnp.float32,
        )
        return product.reshape(mode_dev, nmode, nmom, nmode)

    partial_sums = lax.map(triplet_part, gathered)
    totals = lax.psum(partial_sums, "site")
    triplet = (totals * float(LAT) ** (-1.5)).astype(jnp.bfloat16)
    comb_ids = jnp.arange(ncomb, dtype=jnp.int32)
    mom_ids = jnp.arange(nmom, dtype=jnp.int32)
    spin_ids = jnp.arange(nspin, dtype=jnp.int32)
    own_spins = lax.dynamic_slice_in_dim(spins, lax.axis_index("site") * comb_dev, comb_dev, 0)
    picker = (own_spins[:, :, None] == spin_ids[None, None, :]).astype(jnp.bfloat16)
    chosen = jnp.einsum(
        "cks,tsmn->tckmn", picker, perams, preferred_element_type=jnp.float32
    ).astype(jnp.bfloat16)
    first = jnp.einsum(
        "tijpk,tcmk->tcijpm", triplet, chosen[:, :, 2], preferred_element_type=jnp.float32
    ).astype(jnp.bfloat16)
    second = jnp.einsum(
        "tcmj,tcijpk->itcpmk", chosen[:, :, 1], first, preferred_element_type=jnp.float32
    ).astype(jnp.bfloat16)
    rows_sel = chosen[:, :, 0]
    cols_sel = lax.dynamic_slice_in_dim(rows_sel, first_mode, mode_dev, 3)
    own_blocks = lax.psum_scatter(
        jnp.einsum("tcmi,itcpjk->mtcpjk", cols_sel, second, preferred_element_type=jnp.float32),
        "mode",
        scatter_dimension=0,
        tiled=True,
    ).astype(jnp.bfloat16)
    all_blocks = lax.all_gather(own_blocks, "site", axis=2, tiled=True)
    swapped = lax.all_to_all(all_blocks, "mode", split_axis=4, concat_axis=0, tiled=True)
    pick_left = (
        (pair_combs[:, 0][:, None, None] == comb_ids[None, :, None])
        & (pair_moms[:, 0][:, None, None] == mom_ids[None, None, :])
    ).astype(jnp.bfloat16)
    pick_right = (
        (pair_combs[:, 1][:, None, None] == comb_ids[None, :, None])
        & (pair_moms[:, 1][:, None, None] == mom_ids[None, None, :])
    ).astype(jnp.bfloat16)
    left_block = jnp.einsum(
        "qcp,itcpjk->qtijk", pick_left, all_blocks, preferred_element_type=jnp.float32
    ).astype(jnp.bfloat16)
    right_block = jnp.einsum(
        "qcp,mtcpnk->qtmnk", pick_right, swapped, preferred_element_type=jnp.float32
    ).astype(jnp.bfloat16)
    partial_corr = jnp.einsum(
        "qtijk,qtjil->qtkl", left_block, right_block, preferred_element_type=jnp.float32
    ) * (1.0 / nmode)
    return lax.psum_scatter(
        partial_corr.astype(jnp.bfloat16), "mode", scatter_dimension=2, tiled=True
    ).astype(jnp.float32)


def solution(mesh):
    placed = (P(None, "mode", None, "site"), P(), P(), P(), P("site", None), P("site", None))
    return jax.shard_map(
        body, mesh=mesh, in_specs=placed, out_specs=P("site", None, "mode", None), check_vma=False
    )
```

profile of v0, /device:TPU:38, one launch (start us, length us, event | category | flops | bytes accessed | tf_op | source)
XLA Modules:
  0.0 601.7 jit_solution(13482562929319963017)
XLA Ops:
  6.5 2.0 copy.22
  8.7 0.9 dynamic-slice_reduce_fusion
  9.5 1.0 slice_reduce_fusion
  10.6 0.4 fusion.23
  11.1 64.4 %all-gather.3.cloned.1.call-done = bf16[2,64,3,6912]{3,0,2,1:T(2,128)(2,1)} async-done(((bf16[2,4,3,6912]{3,0,2,1:T(2,128)(2,1)}), bf16[2,64,3,6912]{3,0,2,1:T(2,128)(2,1)}) %all-gather.3.cloned.1.call-update) | async-done | bytes 5308432 | tf_op jit(solution)/shard_map/all_gather | solution.py:30
  75.5 5.4 copy.23
  80.9 20.2 %while.13 = (s32[]{:T(128)}, f32[2,4,64,2,64]{4,2,3,1,0:T(8,128)S(1)}, bf16[2,64,3,6912]{3,1,2,0:T(8,128)(2,1)}, s32[]{:T(128)}, s32[6912]{0:T(1024)S(1)}, /*ind...) while((s32[]{:T(128)}, ...), condition=%wide.region_1.2_spmd.clone, body=%wide.region_0.1_spmd.clone.sunk | while | flops 1418867712 | bytes 57853072 | solution.py:52
  80.9 2.4 dynamic-slice_convert_fusion.3
  83.4 0.3 slice_bitcast_fusion.8
  83.8 3.2 subtract_convert_fusion.4
  86.9 1.0 sine_add_fusion.2
  88.0 3.0 fusion.62
  91.0 2.4 dynamic-slice_convert_fusion.3
  93.5 0.3 slice_bitcast_fusion.8
  93.9 3.2 subtract_convert_fusion.4
  97.0 1.0 sine_add_fusion.2
  98.1 3.0 fusion.62
  101.1 0.8 copy-done.2
  101.9 0.1 fusion.54
  102.1 0.1 constant_dynamic-slice_fusion
  102.3 135.7 %all-reduce.3.cloned.1.call-done = f32[2,4,64,2,64]{4,2,3,1,0:T(8,128)} async-done(((f32[2,4,64,2,64]{4,2,3,1,0:T(8,128)}), f32[2,4,64,2,64]{4,2,3,1,0:T(8,128)}) %all-reduce.3.cloned.1.call-update) | async-done | bytes 262160 | tf_op jit(solution)/shard_map/psum | solution.py:53
  238.1 1.6 fusion.22
  239.6 0.2 copy.25
  239.8 4.9 convolution_bitcast_fusion
  244.8 9.1 %copy.26 = f32[64,2,1,2,64,64]{5,4,3,2,1,0:T(8,128)} copy(f32[64,2,1,2,64,64]{0,5,4,3,1,2:T(8,128)} %convolution_bitcast_fusion) | data formatting | bytes 8388608 | tf_op jit(solution)/shard_map/tcmi,itcpjk->mtcpjk/transpose | solution.py:72
  253.9 0.2 all-gather.5.cloned.1.call-start
  254.1 109.6 %reduce-scatter.3.cloned.1.call-done = f32[4,2,1,2,64,64]{5,4,3,2,1,0:T(8,128)} async-done(((f32[64,2,1,2,64,64]{5,4,3,2,1,0:T(8,128)}), f32[4,2,1,2,64,64]{5,4,3,2,1,0:T(8,128)}) %reduce-scatter.3.cloned.1.call-update) | async-done | bytes 262160 | tf_op jit(solution)/shard_map/reduce_scatter | solution.py:71
  363.7 1.8 convert_bitcast_fusion
  365.5 99.9 %all-gather.5.cloned.1.call-done = bf16[4,2,16,2,64,64]{5,4,3,1,0,2:T(8,128)(2,1)} async-done(((bf16[4,2,1,2,64,64]{5,4,3,1,0,2:T(8,128)(2,1)}), bf16[4,2,16,2,64,64]{5,4,3,1,0,2:T(8,128)(2,1)}) %all-gather.5.cloned.1.call-update) | async-done | bytes 2097168 | tf_op jit(solution)/shard_map/all_gather | solution.py:77
  465.4 6.9 %copy.74 = bf16[4,2,16,2,64,64]{5,2,3,1,0,4:T(8,128)(2,1)} copy(bf16[4,2,16,2,64,64]{5,4,3,1,0,2:T(8,128)(2,1)} %all-gather.5.cloned.1.call-done) | data formatting | bytes 4194304 | tf_op jit(solution)/shard_map/all_gather | solution.py:77
  472.3 7.6 %reshape.298 = bf16[16,2,32768]{2,1,0:T(2,128)(2,1)} reshape(bf16[64,4,2,2,16,64]{5,4,3,2,1,0:T(8,128)(2,1)} %bitcast.161) | data formatting | bytes 4194304
  479.9 7.3 %all-to-all-start = ((bf16[16,2,32768]{2,1,0:T(2,128)(2,1)}), bf16[16,2,32768]{2,1,0:T(2,128)(2,1)S(1)}, u32[]{:S(2)}, u32[]{:S(2)}) async-start(bf16[16,2,32768]{2,1,0:T(2,128)(2,1)} %reshape.298), calls=%async_computation.1 | async-start | bytes 4194304 | tf_op jit(solution)/shard_map/all_to_all | solution.py:78
  487.2 0.6 dynamic-slice.2
  488.4 0.6 fusion.56
  489.0 0.6 iota_compare_fusion.1
  489.7 0.6 fusion.55
  490.3 0.6 iota_compare_fusion.2
  490.9 0.6 iota_compare_fusion.3
  491.5 0.7 iota_compare_fusion.4
  492.3 3.4 multiply_reduce_fusion
  495.7 0.1 copy.43
  495.8 18.6 %all-to-all-done = bf16[16,2,32768]{2,1,0:T(2,128)(2,1)S(1)} async-done(((bf16[16,2,32768]{2,1,0:T(2,128)(2,1)}), bf16[16,2,32768]{2,1,0:T(2,128)(2,1)S(1)}, u32[]{:S(2)}, u32[]{:S(2)}) %all-to-all-start) | async-done | bytes 2097184 | tf_op jit(solution)/shard_map/all_to_all | solution.py:78
  514.4 5.0 reshape.299
  519.4 3.4 copy.30
  522.8 0.7 convolution_bitcast_fusion.1
  523.5 0.2 fusion.26
  523.8 70.8 %all-reduce = bf16[1,2,64,64]{3,2,1,0:T(8,128)(2,1)S(1)} all-reduce(bf16[1,2,64,64]{3,2,1,0:T(8,128)(2,1)S(1)} %fusion.26), channel_id=3, replica_groups=mesh['mode'=16,'site'=16] {'mode'}, use_global_device_ids=true, to_apply=%region_4.5.clone | all-reduce | flops 8192 | bytes 32768
  594.5 0.6 dynamic-slice_convert_fusion.1
  (28 shorter events, 0.7 us)
Async XLA Ops:
  6.5 4.1 copy-start
  6.5 68.9 %all-gather.3.cloned.1.call-start = ((), (), s32[]{:S(2)}) async-start(), calls=%async_computation.2 | async-start | bytes 5640192 | tf_op jit(solution)/shard_map/all_gather | solution.py:30
  8.6 229.5 %all-reduce.3.cloned.1.call-start = ((), (), s32[]{:S(2)}) async-start(), calls=%async_computation.3 | async-start | bytes 1048576 | tf_op jit(solution)/shard_map/psum | solution.py:53
  101.1 0.8 copy-start.2
  101.9 261.8 %reduce-scatter.3.cloned.1.call-start = ((), (), s32[]{:S(2)}) async-start(), calls=%async_computation.4 | async-start | bytes 8912896 | tf_op jit(solution)/shard_map/reduce_scatter | solution.py:71
  253.9 211.5 %all-gather.5.cloned.1.call-start = ((), (), s32[]{:S(2)}) async-start(), calls=%async_computation.5 | async-start | bytes 4456448 | tf_op jit(solution)/shard_map/all_gather | solution.py:77
  472.3 14.9 %copy-start.5 = (u32[256]{0:T(256)S(1)}, u32[256]{0:T(256)}, u32[]{:S(2)}) copy-start(u32[256]{0:T(256)} %constant.88) | copy-start | bytes 3076
  472.3 16.1 %copy-start.3 = (s32[1,2]{1,0:T(1,128)S(1)}, s32[1,2]{1,0:T(1,128)}, u32[]{:S(2)}) copy-start(s32[1,2]{1,0:T(1,128)} %param.13) | copy-start | bytes 28
  472.3 17.3 %copy-start.4 = (s32[1,2]{1,0:T(1,128)S(1)}, s32[1,2]{1,0:T(1,128)}, u32[]{:S(2)}) copy-start(s32[1,2]{1,0:T(1,128)} %param.12) | copy-start | bytes 28
  479.9 34.5 %all-to-all-start = ((bf16[16,2,32768]{2,1,0:T(2,128)(2,1)}), bf16[16,2,32768]{2,1,0:T(2,128)(2,1)S(1)}, u32[]{:S(2)}, u32[]{:S(2)}) async-start(bf16[16,2,32768]{2,1,0:T(2,128)(2,1)} %reshape.298), calls=%async_computation.1 | async-start | bytes 4194304 | tf_op jit(solution)/shard_map/all_to_all | solution.py:78
  519.4 75.7 %copy-start.1 = (bf16[2,16,64,64]{3,2,1,0:T(8,128)(2,1)S(1)}, bf16[2,16,64,64]{3,2,1,0:T(8,128)(2,1)}, u32[]{:S(2)}) copy-start(bf16[2,16,64,64]{3,2,1,0:T(8,128)(2,1)} %param.9) | copy-start | bytes 786436
Sparse Core Ops, SparseCore 0:
  10.0 65.4 all-gather.2
  102.0 136.0 all-reduce.2
  254.0 109.6 reduce-scatter.2
  365.6 99.7 all-gather.4
where the time goes:
time: 602 us
  waiting for transfers between devices  428 us (71%)
  blocking collectives  70.8 us (12%)
  local copies, waits for them, and re-layouts  45.4 us (8%)
  other arithmetic  21.7 us (4%)
  between operations  13.9 us (2%)
  matrix products  13.8 us (2%)
  starting transfers between devices  7.58 us (1%)
    psum x1, waiting for transfers between devices, body(): totals = lax.psum(partial_sums, 'site')  136 us
    reduce_scatter x1, waiting for transfers between devices, body(): lax.psum_scatter(jnp.einsum('tcmi,itcpjk->mtcpjk', cols_sel, second, pref...  110 us
    all_gather x1, waiting for transfers between devices, body(): all_blocks = lax.all_gather(own_blocks, 'site', axis=2, tiled=True)  99.9 us
    unnamed x1, blocking collectives  70.8 us
    all_gather x1, waiting for transfers between devices, body(): gathered = lax.all_gather(eigvecs, 'mode', axis=1, tiled=True)  64.4 us
    unnamed x17, local copies, waits for them, and re-layouts  21.4 us
    all_to_all x1, waiting for transfers between devices, body(): lax.all_to_all(all_blocks, 'mode', split_axis=4, concat_axis=0, tiled=True)  18.6 us
  transfers between devices with their start and end apart: 5, of which 5 were waited for; matrix products, arithmetic and copies ran while one was open for 2% of the time, Pallas kernels for 0%

commit v1 on v0

--- a/solution.py
+++ b/solution.py
@@ -50,7 +50,7 @@
         return product.reshape(mode_dev, nmode, nmom, nmode)
 
     partial_sums = lax.map(triplet_part, gathered)
-    totals = lax.psum(partial_sums, "site")
+    totals = jnp.sum(lax.all_gather(partial_sums, "site"), axis=0)
     triplet = (totals * float(LAT) ** (-1.5)).astype(jnp.bfloat16)
     comb_ids = jnp.arange(ncomb, dtype=jnp.int32)
     mom_ids = jnp.arange(nmom, dtype=jnp.int32)

time: 602 us -> 651 us (1.081)
  waiting for transfers between devices: 428 us -> 474 us
    all_gather x0 -> x1, waiting for transfers between devices: none -> 182 us  [body(): totals = jnp.sum(lax.all_gather(partial_sums, 'site'), axis=0)]
    psum x1 -> x0, waiting for transfers between devices: 136 us -> none  [body(): totals = lax.psum(partial_sums, 'site')]
where the time goes in v1:
time: 651 us; the launch traced here: 650 us
  waiting for transfers between devices  474 us (73%)
  blocking collectives  70.8 us (11%)
  local copies, waits for them, and re-layouts  44.7 us (7%)
  other arithmetic  26.2 us (4%)
  between operations  13.9 us (2%)
  matrix products  12.8 us (2%)
  starting transfers between devices  7.58 us (1%)
    all_gather x1, waiting for transfers between devices, body(): totals = jnp.sum(lax.all_gather(partial_sums, 'site'), axis=0)  182 us
    reduce_scatter x1, waiting for transfers between devices, body(): lax.psum_scatter(jnp.einsum('tcmi,itcpjk->mtcpjk', cols_sel, second, pref...  108 us
    all_gather x1, waiting for transfers between devices, body(): all_blocks = lax.all_gather(own_blocks, 'site', axis=2, tiled=True)  100 us
    unnamed x1, blocking collectives  70.8 us
    all_gather x1, waiting for transfers between devices, body(): gathered = lax.all_gather(eigvecs, 'mode', axis=1, tiled=True)  65.7 us
    unnamed x17, local copies, waits for them, and re-layouts  21.4 us
    all_to_all x1, waiting for transfers between devices, body(): lax.all_to_all(all_blocks, 'mode', split_axis=4, concat_axis=0, tiled=True)  18.6 us
  transfers between devices with their start and end apart: 5, of which 5 were waited for; matrix products, arithmetic and copies ran while one was open for 2% of the time, Pallas kernels for 0%

profile of v1, /device:TPU:38, one launch (start us, length us, event | category | flops | bytes accessed | tf_op | source)
XLA Modules:
  0.0 650.4 jit_solution(5910338777041025295)
XLA Ops:
  6.5 2.0 copy.22
  8.7 1.0 slice_reduce_fusion
  9.8 65.7 %all-gather.5.cloned.1.call-done = bf16[2,64,3,6912]{3,0,2,1:T(2,128)(2,1)} async-done(((bf16[2,4,3,6912]{3,0,2,1:T(2,128)(2,1)}), bf16[2,64,3,6912]{3,0,2,1:T(2,128)(2,1)}) %all-gather.5.cloned.1.call-update) | async-done | bytes 5308432 | tf_op jit(solution)/shard_map/all_gather | solution.py:30
  75.5 5.4 copy.23
  80.9 20.2 %while.13 = (s32[]{:T(128)}, f32[2,4,64,2,64]{4,2,3,1,0:T(8,128)S(1)}, bf16[2,64,3,6912]{3,1,2,0:T(8,128)(2,1)}, s32[]{:T(128)}, s32[6912]{0:T(1024)S(1)}, /*ind...) while((s32[]{:T(128)}, ...), condition=%wide.region_1.2_spmd.clone, body=%wide.region_0.1_spmd.clone.sunk | while | flops 1418867712 | bytes 57853072 | solution.py:52
  80.9 2.4 dynamic-slice_convert_fusion.3
  83.4 0.3 slice_bitcast_fusion.8
  83.8 3.2 subtract_convert_fusion.4
  87.0 1.0 sine_add_fusion.2
  88.0 3.0 fusion.62
  91.0 2.4 dynamic-slice_convert_fusion.3
  93.5 0.3 slice_bitcast_fusion.8
  93.9 3.2 subtract_convert_fusion.4
  97.1 1.0 sine_add_fusion.2
  98.1 3.0 fusion.62
  101.1 0.8 copy-done.1
  101.9 0.2 reduce-scatter.3.cloned.1.call-start
  102.2 0.2 dynamic-slice_reduce_fusion
  102.4 0.4 fusion.23
  102.8 0.1 fusion.54
  102.9 0.1 constant_dynamic-slice_fusion
  103.2 181.8 %all-gather.9.cloned.1.call-done = f32[32,4,64,2,64]{4,2,3,1,0:T(8,128)} async-done(((f32[2,4,64,2,64]{4,2,3,1,0:T(8,128)}), f32[32,4,64,2,64]{4,2,3,1,0:T(8,128)}) %all-gather.9.cloned.1.call-update) | async-done | bytes 4194320 | tf_op jit(solution)/shard_map/all_gather | solution.py:53
  285.0 4.4 reduce_sum.9
  289.5 0.5 fusion.22
  290.0 0.2 copy.25
  290.2 4.9 convolution_bitcast_fusion
  295.1 9.1 %copy.26 = f32[64,2,1,2,64,64]{5,4,3,2,1,0:T(8,128)} copy(f32[64,2,1,2,64,64]{0,5,4,3,1,2:T(8,128)} %convolution_bitcast_fusion) | data formatting | bytes 8388608 | tf_op jit(solution)/shard_map/tcmi,itcpjk->mtcpjk/transpose | solution.py:72
  304.3 108.2 %reduce-scatter.3.cloned.1.call-done = f32[4,2,1,2,64,64]{5,4,3,2,1,0:T(8,128)} async-done(((f32[64,2,1,2,64,64]{5,4,3,2,1,0:T(8,128)}), f32[4,2,1,2,64,64]{5,4,3,2,1,0:T(8,128)}) %reduce-scatter.3.cloned.1.call-update) | async-done | bytes 262160 | tf_op jit(solution)/shard_map/reduce_scatter | solution.py:71
  412.5 1.8 convert_bitcast_fusion
  414.3 100.0 %all-gather.7.cloned.1.call-done = bf16[4,2,16,2,64,64]{5,4,3,1,0,2:T(8,128)(2,1)} async-done(((bf16[4,2,1,2,64,64]{5,4,3,1,0,2:T(8,128)(2,1)}), bf16[4,2,16,2,64,64]{5,4,3,1,0,2:T(8,128)(2,1)}) %all-gather.7.cloned.1.call-update) | async-done | bytes 2097168 | tf_op jit(solution)/shard_map/all_gather | solution.py:77
  514.3 6.9 %copy.74 = bf16[4,2,16,2,64,64]{5,2,3,1,0,4:T(8,128)(2,1)} copy(bf16[4,2,16,2,64,64]{5,4,3,1,0,2:T(8,128)(2,1)} %all-gather.7.cloned.1.call-done) | data formatting | bytes 4194304 | tf_op jit(solution)/shard_map/all_gather | solution.py:77
  521.2 7.6 %reshape.299 = bf16[16,2,32768]{2,1,0:T(2,128)(2,1)} reshape(bf16[64,4,2,2,16,64]{5,4,3,2,1,0:T(8,128)(2,1)} %bitcast.162) | data formatting | bytes 4194304
  528.7 7.3 %all-to-all-start = ((bf16[16,2,32768]{2,1,0:T(2,128)(2,1)}), bf16[16,2,32768]{2,1,0:T(2,128)(2,1)S(1)}, u32[]{:S(2)}, u32[]{:S(2)}) async-start(bf16[16,2,32768]{2,1,0:T(2,128)(2,1)} %reshape.299), calls=%async_computation.1 | async-start | bytes 4194304 | tf_op jit(solution)/shard_map/all_to_all | solution.py:78
  536.0 0.6 dynamic-slice.2
  537.2 0.6 fusion.56
  537.8 0.6 iota_compare_fusion.1
  538.5 0.6 fusion.55
  539.1 0.6 iota_compare_fusion.2
  539.7 0.6 iota_compare_fusion.3
  540.4 0.7 iota_compare_fusion.4
  541.2 3.4 multiply_reduce_fusion
  544.7 18.6 %all-to-all-done = bf16[16,2,32768]{2,1,0:T(2,128)(2,1)S(1)} async-done(((bf16[16,2,32768]{2,1,0:T(2,128)(2,1)}), bf16[16,2,32768]{2,1,0:T(2,128)(2,1)S(1)}, u32[]{:S(2)}, u32[]{:S(2)}) %all-to-all-start) | async-done | bytes 2097184 | tf_op jit(solution)/shard_map/all_to_all | solution.py:78
  563.3 5.0 reshape.300
  568.2 3.3 copy.30
  571.6 0.7 convolution_bitcast_fusion.1
  572.3 0.2 fusion.26
  572.5 70.8 %all-reduce = bf16[1,2,64,64]{3,2,1,0:T(8,128)(2,1)S(1)} all-reduce(bf16[1,2,64,64]{3,2,1,0:T(8,128)(2,1)S(1)} %fusion.26), channel_id=4, replica_groups=mesh['mode'=16,'site'=16] {'mode'}, use_global_device_ids=true, to_apply=%region_4.5.clone | all-reduce | flops 8192 | bytes 32768
  643.3 0.6 dynamic-slice_convert_fusion.1
  (29 shorter events, 0.8 us)
Async XLA Ops:
  6.5 95.8 %copy-start = (bf16[2,16,64,64]{3,2,1,0:T(8,128)(2,1)S(1)}, bf16[2,16,64,64]{3,2,1,0:T(8,128)(2,1)}, u32[]{:S(2)}) copy-start(bf16[2,16,64,64]{3,2,1,0:T(8,128)(2,1)} %param.9) | copy-start | bytes 786436
  6.5 68.9 %all-gather.5.cloned.1.call-start = ((), (), s32[]{:S(2)}) async-start(), calls=%async_computation.2 | async-start | bytes 5640192 | tf_op jit(solution)/shard_map/all_gather | solution.py:30
  8.6 276.4 %all-gather.9.cloned.1.call-start = ((), (), s32[]{:S(2)}) async-start(), calls=%async_computation.5 | async-start | bytes 8912896 | tf_op jit(solution)/shard_map/all_gather | solution.py:53
  80.9 21.3 %copy-start.2 = (s32[16,3]{0,1:T(4,128)S(1)}, s32[16,3]{0,1:T(4,128)}, u32[]{:S(2)}) copy-start(s32[16,3]{0,1:T(4,128)} %param.11) | copy-start | bytes 580
  101.1 0.8 copy-start.1
  101.9 310.6 %reduce-scatter.3.cloned.1.call-start = ((), (), s32[]{:S(2)}) async-start(), calls=%async_computation.3 | async-start | bytes 8912896 | tf_op jit(solution)/shard_map/reduce_scatter | solution.py:71
  304.2 210.0 %all-gather.7.cloned.1.call-start = ((), (), s32[]{:S(2)}) async-start(), calls=%async_computation.4 | async-start | bytes 4456448 | tf_op jit(solution)/shard_map/all_gather | solution.py:77
  521.1 14.9 %copy-start.5 = (u32[256]{0:T(256)S(1)}, u32[256]{0:T(256)}, u32[]{:S(2)}) copy-start(u32[256]{0:T(256)} %constant.89) | copy-start | bytes 3076
  521.1 16.1 %copy-start.3 = (s32[1,2]{1,0:T(1,128)S(1)}, s32[1,2]{1,0:T(1,128)}, u32[]{:S(2)}) copy-start(s32[1,2]{1,0:T(1,128)} %param.13) | copy-start | bytes 28
  521.1 17.3 %copy-start.4 = (s32[1,2]{1,0:T(1,128)S(1)}, s32[1,2]{1,0:T(1,128)}, u32[]{:S(2)}) copy-start(s32[1,2]{1,0:T(1,128)} %param.12) | copy-start | bytes 28
  528.7 34.5 %all-to-all-start = ((bf16[16,2,32768]{2,1,0:T(2,128)(2,1)}), bf16[16,2,32768]{2,1,0:T(2,128)(2,1)S(1)}, u32[]{:S(2)}, u32[]{:S(2)}) async-start(bf16[16,2,32768]{2,1,0:T(2,128)(2,1)} %reshape.299), calls=%async_computation.1 | async-start | bytes 4194304 | tf_op jit(solution)/shard_map/all_to_all | solution.py:78
Sparse Core Ops, SparseCore 0:
  10.0 65.4 all-gather.4
  102.0 182.9 all-gather.8
  304.4 108.1 reduce-scatter.2
  414.5 99.7 all-gather.6
